TPU v7x, 256 devices: a whole 4x4x8 slice. The times are simulated.
256 devices in a mesh: pts: 8 (over z_lo, core), coord: 32 (over y, z_hi, x).
Axes of the slice: x: 4, y: 4, z: 8 (z_hi: 2, z_lo: 4; z = z_hi * 4 + z_lo), core: 2. Of those that a mesh axis runs over, the one named last changes fastest.
Arguments:
- point_seed: int32 [512], P('pts'), may hold values from 0 to 16777215
- pert_seed: int32 [512, 16], P('pts'), may hold values from 0 to 16777215
- source_coef: float32 [100000], P('coord'), may hold values from -9 to 9
- w1: bfloat16 [1024, 100000], P(None, 'coord'), may hold values from -0.009765625 to 0.009765625
- b1: float32 [1024], replicated, may hold values from -3 to 3
- w2: bfloat16 [1024, 1024], replicated, may hold values from -0.1875 to 0.1875
- w3: bfloat16 [1024], replicated, may hold values from -0.1875 to 0.1875
Outputs:
- residual: float32 [512], P(('pts', 'coord'))
- grad_w1: bfloat16 [1024, 100000], P('pts', 'coord')
- grad_w2: float32 [1024, 1024], P('coord')
- grad_b1: float32 [1024], P('coord')
- grad_w3: float32 [1024], P('coord')
All inputs are finite; a program needn't handle non-finite values.
Results may differ from a plain program's by a relative error of at most 0.023.
Values may be sent and summed in bfloat16 or wider, within the bound.
A program may use at most 128 MiB of HBM per device.

v0:
```python
import math
import jax
import jax.numpy as jnp
from jax import lax
from jax.sharding import PartitionSpec as P

D = 100000
hash_factor = 73244475
NOISE_SCALE = 2.0
READOUT = 0.0625


def shuffle_bits(packed_bits):
    return packed_bits ^ lax.shift_right_logical(packed_bits, jnp.full_like(packed_bits, 16))


def mix_bits(packed_bits):
    packed_bits = shuffle_bits(packed_bits)
    packed_bits = shuffle_bits(packed_bits * hash_factor)
    return shuffle_bits(packed_bits * hash_factor)


def to_unit(packed_bits):
    return ((packed_bits & 8388607).astype(jnp.float32) + 0.5) * (1.0 / 8388608.0)


def column_keys(columns):
    return (mix_bits(columns * 4), mix_bits(columns * 4 + 1), mix_bits(columns * 4 + 2))


def perturbed_rows(point_seeds, pert_seeds, column_hash, coef_part):
    key_zero, key_one, key_two = column_hash
    count_points, count_samples = pert_seeds.shape
    uniform_point = to_unit(mix_bits(key_two[None, :] ^ point_seeds[:, None]))
    coords = 2.0 * uniform_point - 1.0
    uniform_zero = to_unit(mix_bits(key_zero[None, None, :] ^ pert_seeds[:, :, None]))
    uniform_one = to_unit(mix_bits(key_one[None, None, :] ^ pert_seeds[:, :, None]))
    noise_draw = jnp.sqrt(-2.0 * jnp.log(uniform_zero)) * jnp.cos(2.0 * jnp.pi * uniform_one)
    shifted = (coords[:, None, :] + NOISE_SCALE * noise_draw).astype(jnp.bfloat16)
    shifted = shifted.reshape(count_points * count_samples, coords.shape[1])
    squares = jnp.sum(noise_draw * noise_draw, axis=2).reshape(count_points * count_samples)
    source = jnp.sum(coef_part[None, :] * jnp.sin(jnp.pi * coords), axis=1) / math.sqrt(D)
    return (shifted, squares, source)


def hidden_pass(pre_first, squares, source, w2, w3, count_samples):
    hidden_one = jnp.tanh(pre_first).astype(jnp.bfloat16)
    pre_second = lax.dot_general(
        hidden_one, w2, (((1,), (1,)), ((), ())), preferred_element_type=jnp.float32
    )
    hidden_two = jnp.tanh(pre_second).astype(jnp.bfloat16)
    values_out = READOUT * jnp.dot(hidden_two, w3, preferred_element_type=jnp.float32)
    stein_weight = (squares - D) / (NOISE_SCALE * NOISE_SCALE * count_samples)
    per_point = (stein_weight * values_out).reshape(-1, count_samples)
    residual = jnp.sum(per_point, axis=1) - source
    grad_values = (residual[:, None] * stein_weight.reshape(-1, count_samples)).reshape(-1)
    two_float = hidden_two.astype(jnp.float32)
    grad_readout = READOUT * jnp.sum(grad_values[:, None] * two_float, axis=0)
    grad_pre_two = (
        READOUT
        * grad_values[:, None]
        * w3.astype(jnp.float32)[None, :]
        * (1.0 - two_float * two_float)
    ).astype(jnp.bfloat16)
    grad_second = lax.dot_general(
        grad_pre_two, hidden_one, (((0,), (0,)), ((), ())), preferred_element_type=jnp.float32
    )
    grad_hidden = jnp.dot(grad_pre_two, w2, preferred_element_type=jnp.float32)
    one_float = hidden_one.astype(jnp.float32)
    grad_pre_one = (grad_hidden * (1.0 - one_float * one_float)).astype(jnp.bfloat16)
    grad_bias = jnp.sum(grad_pre_one.astype(jnp.float32), axis=0)
    return (residual, grad_pre_one, grad_second, grad_bias, grad_readout, hidden_one, grad_pre_two)


def shards(point_seed, pert_seed, source_coef, w1, b1, w2, w3):
    coord_count = lax.axis_size("coord")
    coord_width = w1.shape[1]
    points_here, samples = pert_seed.shape
    rows_here = points_here * samples
    rows_local = rows_here // coord_count
    points_local = points_here // coord_count
    coord_index = lax.axis_index("coord")
    columns = coord_index * coord_width + jnp.arange(coord_width, dtype=jnp.int32)
    column_hash = column_keys(columns)
    shifted, squares, source = perturbed_rows(point_seed, pert_seed, column_hash, source_coef)
    picked = shifted
    pre_local = lax.psum_scatter(
        lax.dot_general(picked, w1, (((1,), (1,)), ((), ())), preferred_element_type=jnp.float32),
        "coord",
        scatter_dimension=0,
        tiled=True,
    )
    squares_all, source_all = lax.psum((squares, source), "coord")
    squares_local = lax.dynamic_slice_in_dim(squares_all, coord_index * rows_local, rows_local, 0)
    source_local = lax.dynamic_slice_in_dim(source_all, coord_index * points_local, points_local, 0)
    residual, grad_pre_one, grad_second, grad_bias, grad_readout, hidden_one, grad_pre_two = (
        hidden_pass(pre_local + b1[None, :], squares_local, source_local, w2, w3, samples)
    )
    grad_rows = lax.all_gather(grad_pre_one, "coord", axis=0, tiled=True)
    picked = grad_rows
    grad_first = lax.psum_scatter(
        lax.dot_general(
            picked, shifted, (((0,), (0,)), ((), ())), preferred_element_type=jnp.float32
        ).astype(jnp.bfloat16),
        "pts",
        scatter_dimension=0,
        tiled=True,
    )
    share_second, share_bias, share_readout = (
        lax.psum_scatter(
            grad_second.astype(jnp.bfloat16), "coord", scatter_dimension=0, tiled=True
        ).astype(jnp.float32),
        lax.psum_scatter(
            grad_bias.astype(jnp.bfloat16), "coord", scatter_dimension=0, tiled=True
        ).astype(jnp.float32),
        lax.psum_scatter(
            grad_readout.astype(jnp.bfloat16), "coord", scatter_dimension=0, tiled=True
        ).astype(jnp.float32),
    )
    out_second, out_bias, out_readout = (
        lax.psum(share_second.astype(jnp.bfloat16), "pts").astype(jnp.float32),
        lax.psum(share_bias.astype(jnp.bfloat16), "pts").astype(jnp.float32),
        lax.psum(share_readout.astype(jnp.bfloat16), "pts").astype(jnp.float32),
    )
    return (residual, grad_first, out_second, out_bias, out_readout)


def solution(mesh):
    return jax.shard_map(
        shards,
        mesh=mesh,
        in_specs=(P("pts"), P("pts", None), P("coord"), P(None, "coord"), P(), P(), P()),
        out_specs=(
            P(("pts", "coord")),
            P("pts", "coord"),
            P("coord", None),
            P("coord"),
            P("coord"),
        ),
        check_vma=False,
    )
```

profile of v0, /device:TPU:1, one launch (start us, length us, event | category | flops | bytes accessed | tf_op | source)
XLA Modules:
  0.0 800.5 jit_solution(16428335105259536183)
XLA Ops:
  7.3 0.9 copy.17
  8.3 4.2 multiply_reduce_fusion
  12.5 58.9 %fusion.37 = bf16[1024,3125]{1,0:T(8,128)(2,1)S(1)} fusion(s32[3125]{0:T(1024)S(1)} %get-tuple-element.18, s32[1024]{0:T(1024)S(1)} %xor.202, s32[3125]{0:T(1024)S(1)} %shift-right-logical_xor_fusion.21, f32[64,3125]{1,0:T(8,128)S(1)} %get-tuple-element.14), kind=kLoop, calls=%fused_computation.49 | loop fusion | flops 99200000 | bytes 7229096 | tf_op jit(solution)/shard_map/convert_element_type | solution.py:39
  71.4 2.7 copy-done.5
  74.1 8.8 %fusion.67 = f32[1024,1024]{1,0:T(8,128)} fusion(bf16[1024,3125]{1,0:T(8,128)(2,1)S(1)} %fusion.37, bf16[1024,3125]{0,1:T(8,128)(2,1)S(1)} %bitcast.23), kind=kOutput, calls=%fused_computation.103 | convolution fusion | flops 6553600000 | bytes 16994304 | tf_op jit(solution)/shard_map/dot_general | solution.py:88
  83.1 58.9 %fusion.38 = f32[64,16]{1,0:T(8,128)S(1)} fusion(s32[3125]{0:T(1024)S(1)} %get-tuple-element.18, s32[64,16]{1,0:T(8,128)S(1)} %copy.17, s32[3125]{0:T(1024)S(1)} %shift-right-logical_xor_fusion.21), kind=kLoop, calls=%fused_computation.50 | loop fusion | flops 95998976 | bytes 33192 | tf_op jit(solution)/shard_map/reduce_sum | solution.py:41
  142.0 110.4 %all-reduce.2 = (f32[1024]{0:T(1024)S(1)}, f32[64]{0:T(128)S(1)}) all-reduce(f32[1024]{0:T(1024)S(1)} %reshape.111, f32[64]{0:T(128)S(1)} %broadcast_multiply_fusion), channel_id=1, replica_groups=mesh['pts'=8,'coord'=32] {'coord'}, use_global_device_ids=true, to_apply=%region_1.0 | all-reduce | flops 1088 | bytes 8704 | tf_op jit(solution)/shard_map/psum | solution.py:93
  252.4 49.9 %reduce-scatter.6.cloned.1.call-done = f32[32,1024]{1,0:T(8,128)} async-done(((f32[1024,1024]{1,0:T(8,128)}), f32[32,1024]{1,0:T(8,128)}) %reduce-scatter.6.cloned.1.call-update) | async-done | bytes 131088 | tf_op jit(solution)/shard_map/reduce_scatter | solution.py:87
  302.4 0.9 tanh_convert_fusion
  303.3 0.7 fusion.40
  304.0 0.1 fusion.42
  304.7 2.1 convolution_convert_fusion.1
  306.9 1.1 fusion.66
  308.1 221.3 %reduce-scatter.8.cloned.1.call-done = bf16[32,1024]{1,0:T(8,128)(2,1)} async-done(((bf16[1024,1024]{1,0:T(8,128)(2,1)}), bf16[32,1024]{1,0:T(8,128)(2,1)}) %reduce-scatter.8.cloned.1.call-update) | async-done | bytes 65552 | tf_op jit(solution)/shard_map/reduce_scatter | solution.py:110
  529.5 108.2 %all-gather.2.cloned.1.call-done = bf16[1024,1024]{1,0:T(8,128)(2,1)} async-done(((bf16[32,1024]{1,0:T(8,128)(2,1)}), bf16[1024,1024]{1,0:T(8,128)(2,1)}) %all-gather.2.cloned.1.call-update) | async-done | bytes 2097168 | tf_op jit(solution)/shard_map/all_gather | solution.py:99
  637.7 12.0 %convolution_convert_fusion = bf16[1024,3125]{0,1:T(8,128)(2,1)} fusion(bf16[1024,1024]{1,0:T(8,128)(2,1)} %all-gather.2.cloned.1.call-done, bf16[1024,3125]{1,0:T(8,128)(2,1)} %copy-done.5), kind=kOutput, calls=%fused_computation.51 | convolution fusion | flops 6556800000 | bytes 14897152 | tf_op jit(solution)/shard_map/dot_general | solution.py:102
  649.7 9.2 %copy.19 = bf16[1024,3125]{1,0:T(8,128)(2,1)} copy(bf16[1024,3125]{0,1:T(8,128)(2,1)} %convolution_convert_fusion) | data formatting | bytes 12800000
  658.9 0.6 dynamic-slice
  660.3 96.0 %all-reduce.3 = (bf16[1024]{0:T(1024)(128)(2,1)S(1)}, bf16[1024]{0:T(1024)(128)(2,1)S(1)}) all-reduce(bf16[1024]{0:T(1024)(128)(2,1)S(1)} %get-tuple-element.15, bf16[1024]{0:T(1024)(128)(2,1)S(1)} %multiply_convert_fusion), channel_id=5, replica_groups=mesh['pts'=8,'coord'=32] {'coord'}, use_global_device_ids=true, to_apply=%region_10.0.clone | all-reduce | flops 2048 | bytes 8192
  756.4 32.8 %all-reduce.4 = (bf16[32]{0:T(256)(128)(2,1)S(1)}, bf16[32]{0:T(256)(128)(2,1)S(1)}) all-reduce(bf16[32]{0:T(256)(128)(2,1)S(1)} %dynamic-slice.1, bf16[32]{0:T(256)(128)(2,1)S(1)} %dynamic-slice.3), channel_id=1, replica_groups=mesh['pts'=8,'coord'=32] {'pts'}, use_global_device_ids=true, to_apply=%region_11.0 | all-reduce | flops 64 | bytes 256 | tf_op jit(solution)/shard_map/psum | solution.py:122
  789.2 0.5 convert_element_type.86
  789.7 0.5 convert_element_type.88
  790.3 1.5 convert_element_type.85
  791.8 2.2 copy.20
  (45 shorter events, 1.3 us)
Async XLA Ops:
  7.2 296.1 %copy-start = (bf16[1024,1024]{1,0:T(8,128)(2,1)S(1)}, bf16[1024,1024]{1,0:T(8,128)(2,1)}, u32[]{:S(2)}) copy-start(bf16[1024,1024]{1,0:T(8,128)(2,1)} %param.12) | copy-start | bytes 6291460
  7.2 295.2 %reduce-scatter.6.cloned.1.call-start = ((), (), s32[]{:S(2)}) async-start(), calls=%async_computation.3 | async-start | bytes 4325376 | tf_op jit(solution)/shard_map/reduce_scatter | solution.py:87
  8.3 65.8 %slice-start = ((s8[6406144]{0:T(1024)(128)(4,1)}), s8[4194304]{0:T(1024)(128)(4,1)S(1)}, s32[]{:S(2)}) async-start(s8[6406144]{0:T(1024)(128)(4,1)} %bitcast.22), calls=%async_computation.8 | async-start | bytes 8388608
  12.4 61.7 %slice-start.1 = ((s8[6406144]{0:T(1024)(128)(4,1)}), s8[2211840]{0:T(1024)(128)(4,1)S(1)}, s32[]{:S(2)}) async-start(s8[6406144]{0:T(1024)(128)(4,1)} %bitcast.22), calls=%async_computation.9 | async-start | bytes 4423680
  71.4 2.7 copy-start.5
  74.1 8.9 %copy-start.1 = (bf16[1024]{0:T(1024)(128)(2,1)S(1)}, bf16[1024]{0:T(1024)(128)(2,1)}, u32[]{:S(2)}) copy-start(bf16[1024]{0:T(1024)(128)(2,1)} %param.13) | copy-start | bytes 6148
  83.0 446.5 %reduce-scatter.8.cloned.1.call-start = ((), (), s32[]{:S(2)}) async-start(), calls=%async_computation.5 | async-start | bytes 2162688 | tf_op jit(solution)/shard_map/reduce_scatter | solution.py:110
  83.1 219.3 %copy-start.2 = (f32[1024]{0:T(1024)S(1)}, f32[1024]{0:T(1024)}, u32[]{:S(2)}) copy-start(f32[1024]{0:T(1024)} %param.11) | copy-start | bytes 12292
  304.5 345.2 %copy-start.3 = (f32[2]{0:T(128)}, f32[2]{0:T(128)S(1)}, u32[]{:S(2)}) copy-start(f32[2]{0:T(128)S(1)} %dynamic-slice_subtract_fusion) | copy-start | bytes 28
  306.9 330.8 %all-gather.2.cloned.1.call-start = ((), (), s32[]{:S(2)}) async-start(), calls=%async_computation.4 | async-start | bytes 2162688 | tf_op jit(solution)/shard_map/all_gather | solution.py:99
  308.1 482.2 %all-reduce.7.cloned.1.call-start = ((), (), s32[]{:S(2)}) async-start(), calls=%async_computation.6 | async-start | bytes 131072 | tf_op jit(solution)/shard_map/psum | solution.py:121
  529.5 262.3 %reduce-scatter.10.cloned.1.call-start = ((), (), s32[]{:S(2)}) async-start(), calls=%async_computation.7 | async-start | bytes 7372800
  649.7 9.2 %copy-start.4 = (u32[256]{0:T(256)S(1)}, u32[256]{0:T(256)}, u32[]{:S(2)}) copy-start(u32[256]{0:T(256)} %constant.76) | copy-start | bytes 3076
Sparse Core Ops, SparseCore 0:
  83.1 219.1 reduce-scatter.5
  307.0 222.4 reduce-scatter.7
  533.5 104.0 all-gather.1
  640.1 66.6 all-reduce.6
  709.2 77.9 reduce-scatter.9
where the time goes:
time: 801 us; the launch traced here: 800 us
  waiting for transfers between devices  379 us (47%)
  blocking collectives  239 us (30%)
  other arithmetic  126 us (16%)
  matrix products  25 us (3%)
  local copies, waits for them, and re-layouts  16.2 us (2%)
  between operations  14.6 us (2%)
    reduce_scatter x1, waiting for transfers between devices, shards(): lax.psum_scatter(grad_second.astype(jnp.bfloat16), 'coord', scatter_dimen...  221 us
    psum x1, blocking collectives, shards(): squares_all, source_all = lax.psum((squares, source), 'coord')  110 us
    all_gather x1, waiting for transfers between devices, shards(): grad_rows = lax.all_gather(grad_pre_one, 'coord', axis=0, tiled=True)  108 us
    unnamed x1, blocking collectives  96 us
    convert_element_type x1, other arithmetic, perturbed_rows(): (coords[:, None, :] + NOISE_SCALE * noise_draw).astype(jnp.bfloat16)  58.9 us
    reduce_sum x1, other arithmetic, perturbed_rows(): jnp.sum(noise_draw * noise_draw, axis=2)  58.9 us
    reduce_scatter x1, waiting for transfers between devices, shards(): lax.psum_scatter(lax.dot_general(picked, w1, (((1,), (1,)), ((), ())), pr...  49.9 us
    psum x1, blocking collectives, shards(): lax.psum(share_bias.astype(jnp.bfloat16), 'pts').astype(jnp.float32)  32.8 us
  transfers between devices with their start and end apart: 5, of which 3 were waited for; matrix products, arithmetic and copies ran while one was open for 11% of the time, Pallas kernels for 0%

commit v1 on v0

--- a/solution.py
+++ b/solution.py
@@ -96,7 +96,9 @@
     residual, grad_pre_one, grad_second, grad_bias, grad_readout, hidden_one, grad_pre_two = (
         hidden_pass(pre_local + b1[None, :], squares_local, source_local, w2, w3, samples)
     )
-    grad_rows = lax.all_gather(grad_pre_one, "coord", axis=0, tiled=True)
+    grad_rows = jnp.concatenate(
+        lax.all_to_all(jnp.stack([grad_pre_one] * lax.axis_size("coord")), "coord", 0, 0), axis=0
+    )
     picked = grad_rows
     grad_first = lax.psum_scatter(
         lax.dot_general(

time: 801 us -> 733 us (0.915)
  waiting for transfers between devices: 379 us -> 284 us
  blocking collectives: 239 us -> 260 us
    all_gather x1 -> x0, waiting for transfers between devices: 108 us -> none  [shards(): grad_rows = lax.all_gather(grad_pre_one, 'coord', axis=0, tiled=True)]
    convert_element_type x1 -> x2, other arithmetic: 58.9 us -> 121 us  [perturbed_rows(): (coords[:, None, :] + NOISE_SCALE * noise_draw).astype(jnp.bfloat16)]
    reduce_sum x1 -> x0, other arithmetic: 58.9 us -> none  [perturbed_rows(): jnp.sum(noise_draw * noise_draw, axis=2)]
    psum x1, blocking collectives: 32.8 us -> 53.5 us  [shards(): lax.psum(share_bias.astype(jnp.bfloat16), 'pts').astype(jnp.float32)]
    reduce_scatter x1, waiting for transfers between devices: 221 us -> 236 us  [shards(): lax.psum_scatter(grad_second.astype(jnp.bfloat16), 'coord', scatter_dimen...]
  transfers between devices with their start and end apart: 5 -> 5, of which waited for: 3 -> 2; matrix products, arithmetic and copies ran while one was open for 11% -> 12% of each run, Pallas kernels for 0% -> 0%
where the time goes in v1:
time: 733 us; the launch traced here: 732 us
  waiting for transfers between devices  284 us (39%)
  blocking collectives  260 us (35%)
  other arithmetic  129 us (18%)
  matrix products  24.5 us (3%)
  local copies, waits for them, and re-layouts  15 us (2%)
  between operations  14.6 us (2%)
    reduce_scatter x1, waiting for transfers between devices, shards(): lax.psum_scatter(grad_second.astype(jnp.bfloat16), 'coord', scatter_dimen...  236 us
    convert_element_type x2, other arithmetic, perturbed_rows(): (coords[:, None, :] + NOISE_SCALE * noise_draw).astype(jnp.bfloat16)  121 us
    psum x1, blocking collectives, shards(): squares_all, source_all = lax.psum((squares, source), 'coord')  110 us
    unnamed x1, blocking collectives  96.8 us
    psum x1, blocking collectives, shards(): lax.psum(share_bias.astype(jnp.bfloat16), 'pts').astype(jnp.float32)  53.5 us
    reduce_scatter x1, waiting for transfers between devices, shards(): lax.psum_scatter(lax.dot_general(picked, w1, (((1,), (1,)), ((), ())), pr...  47.8 us
  transfers between devices with their start and end apart: 5, of which 2 were waited for; matrix products, arithmetic and copies ran while one was open for 12% of the time, Pallas kernels for 0%

profile of v1, /device:TPU:1, one launch (start us, length us, event | category | flops | bytes accessed | tf_op | source)
XLA Modules:
  0.0 732.0 jit_solution(5503498493576188559)
XLA Ops:
  7.3 0.9 copy.17
  8.3 4.2 multiply_reduce_fusion.1
  12.5 58.9 %fusion.36 = bf16[1024,3125]{1,0:T(8,128)(2,1)S(1)} fusion(s32[3125]{0:T(1024)S(1)} %get-tuple-element.20, s32[1024]{0:T(1024)S(1)} %xor.258, s32[3125]{0:T(1024)S(1)} %shift-right-logical_xor_fusion.21, f32[64,3125]{1,0:T(8,128)S(1)} %get-tuple-element.16), kind=kLoop, calls=%fused_computation.49 | loop fusion | flops 99200000 | bytes 7229096 | tf_op jit(solution)/shard_map/convert_element_type | solution.py:39
  71.4 8.8 %fusion.65 = f32[1024,1024]{1,0:T(8,128)} fusion(bf16[1024,3125]{1,0:T(8,128)(2,1)S(1)} %fusion.36, bf16[1024,3125]{0,1:T(8,128)(2,1)S(1)} %bitcast.25), kind=kOutput, calls=%fused_computation.103 | convolution fusion | flops 6553600000 | bytes 16994304 | tf_op jit(solution)/shard_map/dot_general | solution.py:88
  80.4 61.9 %add_convert_fusion = (bf16[64,16,3125]{2,1,0:T(8,128)(2,1)}, f32[64,16]{1,0:T(8,128)S(1)}) fusion(f32[64,3125]{1,0:T(8,128)S(1)} %get-tuple-element.16, s32[3125]{0:T(1024)S(1)} %get-tuple-element.20, s32[64,16]{1,0:T(8,128)S(1)} %copy.17, s32[3125]{0:T(1024)S(1)} %shift-right-logical_xor_fusion.21), kind=kLoop, calls=%fused_computation.48 | loop fusion | flops 105598976 | bytes 7233192 | tf_op jit(solution)/shard_map/convert_element_type | solution.py:39
  142.3 110.0 %all-reduce.2 = (f32[1024]{0:T(1024)S(1)}, f32[64]{0:T(128)S(1)}) all-reduce(f32[1024]{0:T(1024)S(1)} %reshape.203, f32[64]{0:T(128)S(1)} %broadcast_multiply_fusion), channel_id=1, replica_groups=mesh['pts'=8,'coord'=32] {'coord'}, use_global_device_ids=true, to_apply=%region_1.0 | all-reduce | flops 1088 | bytes 8704 | tf_op jit(solution)/shard_map/psum | solution.py:93
  252.3 47.8 %reduce-scatter.6.cloned.1.call-done = f32[32,1024]{1,0:T(8,128)} async-done(((f32[1024,1024]{1,0:T(8,128)}), f32[32,1024]{1,0:T(8,128)}) %reduce-scatter.6.cloned.1.call-update) | async-done | bytes 131088 | tf_op jit(solution)/shard_map/reduce_scatter | solution.py:87
  300.1 0.9 tanh_convert_fusion
  301.0 0.7 fusion.38
  301.8 0.1 fusion.40
  302.4 2.2 convolution_convert_fusion.1
  304.6 0.5 fusion.64
  305.2 1.6 stack.2
  306.8 4.8 all-to-all-start
  311.6 236.0 %reduce-scatter.8.cloned.1.call-done = bf16[32,1024]{1,0:T(8,128)(2,1)} async-done(((bf16[1024,1024]{1,0:T(8,128)(2,1)}), bf16[32,1024]{1,0:T(8,128)(2,1)}) %reduce-scatter.8.cloned.1.call-update) | async-done | bytes 65552 | tf_op jit(solution)/shard_map/reduce_scatter | solution.py:112
  547.7 12.0 %convolution_convert_fusion = bf16[1024,3125]{0,1:T(8,128)(2,1)} fusion(bf16[1024,1024]{1,0:T(8,128)(2,1)} %bitcast.2, bf16[1024,3125]{1,0:T(8,128)(2,1)} %bitcast.26), kind=kOutput, calls=%fused_computation.51 | convolution fusion | flops 6556800000 | bytes 14897152 | tf_op jit(solution)/shard_map/dot_general | solution.py:104
  559.8 9.2 %copy.19 = bf16[1024,3125]{1,0:T(8,128)(2,1)} copy(bf16[1024,3125]{0,1:T(8,128)(2,1)} %convolution_convert_fusion) | data formatting | bytes 12800000
  569.0 0.6 dynamic-slice
  570.3 96.8 %all-reduce.3 = (bf16[1024]{0:T(1024)(128)(2,1)S(1)}, bf16[1024]{0:T(1024)(128)(2,1)S(1)}) all-reduce(bf16[1024]{0:T(1024)(128)(2,1)S(1)} %get-tuple-element.17, bf16[1024]{0:T(1024)(128)(2,1)S(1)} %multiply_convert_fusion), channel_id=5, replica_groups=mesh['pts'=8,'coord'=32] {'coord'}, use_global_device_ids=true, to_apply=%region_10.0.clone | all-reduce | flops 2048 | bytes 8192
  667.3 53.5 %all-reduce.4 = (bf16[32]{0:T(256)(128)(2,1)S(1)}, bf16[32]{0:T(256)(128)(2,1)S(1)}) all-reduce(bf16[32]{0:T(256)(128)(2,1)S(1)} %dynamic-slice.1, bf16[32]{0:T(256)(128)(2,1)S(1)} %dynamic-slice.3), channel_id=1, replica_groups=mesh['pts'=8,'coord'=32] {'pts'}, use_global_device_ids=true, to_apply=%region_11.0 | all-reduce | flops 64 | bytes 256 | tf_op jit(solution)/shard_map/psum | solution.py:124
  720.8 0.5 convert_element_type.113
  721.3 0.5 convert_element_type.115
  721.8 1.5 convert_element_type.112
  723.3 2.2 copy.20
  (43 shorter events, 1.2 us)
Async XLA Ops:
  7.2 293.9 %copy-start = (bf16[1024,1024]{1,0:T(8,128)(2,1)S(1)}, bf16[1024,1024]{1,0:T(8,128)(2,1)}, u32[]{:S(2)}) copy-start(bf16[1024,1024]{1,0:T(8,128)(2,1)} %param.12) | copy-start | bytes 6291460
  7.2 292.9 %reduce-scatter.6.cloned.1.call-start = ((), (), s32[]{:S(2)}) async-start(), calls=%async_computation.4 | async-start | bytes 4325376 | tf_op jit(solution)/shard_map/reduce_scatter | solution.py:87
  8.3 63.1 %slice-start = ((s8[6406144]{0:T(1024)(128)(4,1)}), s8[4194304]{0:T(1024)(128)(4,1)S(1)}, s32[]{:S(2)}) async-start(s8[6406144]{0:T(1024)(128)(4,1)} %bitcast.24), calls=%async_computation.8 | async-start | bytes 8388608
  12.4 59.0 %slice-start.1 = ((s8[6406144]{0:T(1024)(128)(4,1)}), s8[2211840]{0:T(1024)(128)(4,1)S(1)}, s32[]{:S(2)}) async-start(s8[6406144]{0:T(1024)(128)(4,1)} %bitcast.24), calls=%async_computation.9 | async-start | bytes 4423680
  71.4 8.9 %copy-start.1 = (bf16[1024]{0:T(1024)(128)(2,1)S(1)}, bf16[1024]{0:T(1024)(128)(2,1)}, u32[]{:S(2)}) copy-start(bf16[1024]{0:T(1024)(128)(2,1)} %param.13) | copy-start | bytes 6148
  80.3 467.4 %reduce-scatter.8.cloned.1.call-start = ((), (), s32[]{:S(2)}) async-start(), calls=%async_computation.5 | async-start | bytes 2162688 | tf_op jit(solution)/shard_map/reduce_scatter | solution.py:112
  80.4 219.7 %copy-start.2 = (f32[1024]{0:T(1024)S(1)}, f32[1024]{0:T(1024)}, u32[]{:S(2)}) copy-start(f32[1024]{0:T(1024)} %param.11) | copy-start | bytes 12292
  302.2 257.6 %copy-start.3 = (f32[2]{0:T(128)}, f32[2]{0:T(128)S(1)}, u32[]{:S(2)}) copy-start(f32[2]{0:T(128)S(1)} %dynamic-slice_subtract_fusion) | copy-start | bytes 28
  306.8 241.0 %all-to-all-start = ((bf16[32,32,1024]{2,1,0:T(8,128)(2,1)}), bf16[32,32,1024]{2,1,0:T(8,128)(2,1)}, u32[]{:S(2)}, u32[]{:S(2)}) async-start(bf16[32,32,1024]{2,1,0:T(8,128)(2,1)} %stack.2), calls=%async_computation.1 | async-start | bytes 4194304 | tf_op jit(solution)/shard_map/all_to_all | solution.py:100
  311.5 410.3 %all-reduce.7.cloned.1.call-start = ((), (), s32[]{:S(2)}) async-start(), calls=%async_computation.6 | async-start | bytes 131072 | tf_op jit(solution)/shard_map/psum | solution.py:123
  547.7 175.6 %reduce-scatter.10.cloned.1.call-start = ((), (), s32[]{:S(2)}) async-start(), calls=%async_computation.7 | async-start | bytes 7372800
  559.8 9.2 %copy-start.4 = (u32[256]{0:T(256)S(1)}, u32[256]{0:T(256)}, u32[]{:S(2)}) copy-start(u32[256]{0:T(256)} %constant.76) | copy-start | bytes 3076
Sparse Core Ops, SparseCore 0:
  80.4 219.6 reduce-scatter.5
  304.8 242.8 reduce-scatter.7
  550.3 86.4 all-reduce.6
  639.2 77.7 reduce-scatter.9
